TPU v7x, 256 devices: a whole 4x4x8 slice. The times are simulated.
256 devices in a mesh: ep: 64 (over y, z, core), fs: 4 (over x).
Axes of the slice: x: 4, y: 4, z: 8, core: 2. Of those that a mesh axis runs over, the one named last changes fastest.
Arguments:
- tokens: bfloat16 [8192, 4096], P('ep', 'fs'), may hold values from -6 to 6
- grad_out: bfloat16 [8192, 4096], P('ep', 'fs'), may hold values from -6 to 6
- gate_weight: bfloat16 [4, 14336, 4096], P('fs', 'ep'), may hold values from -0.09375 to 0.09375
- up_weight: bfloat16 [4, 14336, 4096], P('fs', 'ep'), may hold values from -0.09375 to 0.09375
- down_weight: bfloat16 [4, 14336, 4096], P('fs', 'ep'), may hold values from -0.046875 to 0.046875
- gate_values: float32 [4, 256], P('fs'), may hold values from 0.25 to 1
- chosen: int32 [4, 256], replicated, may hold values from 0 to 8191, as said below
- counts: int32 [4], replicated, may hold values from 128 to 256, as said below
Outputs:
- gate_grad: bfloat16 [4, 14336, 4096], P('fs', 'ep')
- up_grad: bfloat16 [4, 14336, 4096], P('fs', 'ep')
- down_grad: bfloat16 [4, 14336, 4096], P('fs', 'ep')
- token_grad: bfloat16 [8192, 4096], P('ep', 'fs')
- score_grad: float32 [4, 256], P('fs')
Inputs may be any that keep to these rules, and one draw needn't show every extreme that they name: `chosen`: the 256 entries of one row are distinct tokens; only the first counts[e] entries of row e are live, the others are padding to be ignored. Among the live entries of one expert at most 6 lie in one aligned block of 128 tokens (the tokens of one index of ep), and in every draw every expert has exactly 6 live entries in some block. `counts`: some expert has all 256 entries live in every draw.
All inputs are finite; a program needn't handle non-finite values.
Results may differ from a plain program's by a relative error of at most 0.0057.
Values may be sent and summed in bfloat16 or wider, within the bound.
No kernel may reach another device: no remote copies, remote signals or barrier semaphores. Data moves between devices by JAX's collectives and lax.ppermute only.
A program may use at most 128 MiB of HBM per device.

v0:
```python
import jax
import jax.numpy as jnp
from jax import lax
from jax.sharding import PartitionSpec as P

SLOTS = 6


def row_products(x_rows, dy_rows, gate_rows, gate_w, up_w, down_w):
    pre_gate = jnp.einsum("rd,hd->rh", x_rows, gate_w, preferred_element_type=jnp.float32)
    pre_up = jnp.einsum("rd,hd->rh", x_rows, up_w, preferred_element_type=jnp.float32)
    sigmoid_val = jax.nn.sigmoid(pre_gate)
    swished = pre_gate * sigmoid_val
    active = (swished * pre_up).astype(jnp.bfloat16)
    probes = jnp.einsum("rd,hd->rh", dy_rows, down_w, preferred_element_type=jnp.float32)
    score_term = jnp.sum(active.astype(jnp.float32) * probes, axis=1)
    weighted = (gate_rows[:, None] * dy_rows.astype(jnp.float32)).astype(jnp.bfloat16)
    d_active = gate_rows[:, None] * probes
    d_gate = (d_active * pre_up * sigmoid_val * (1.0 + pre_gate * (1.0 - sigmoid_val))).astype(
        jnp.bfloat16
    )
    d_up = (d_active * swished).astype(jnp.bfloat16)
    return (active, weighted, d_gate, d_up, score_term)


def weight_grads(stored):
    x_store, weighted_store, active_store, gate_store, up_store = (
        stored[0],
        stored[1],
        stored[2],
        stored[3],
        stored[4],
    )
    grad_g = jnp.einsum("rh,rd->hd", gate_store, x_store, preferred_element_type=jnp.float32)
    grad_u = jnp.einsum("rh,rd->hd", up_store, x_store, preferred_element_type=jnp.float32)
    grad_d = jnp.einsum(
        "rh,rd->hd", active_store, weighted_store, preferred_element_type=jnp.float32
    )
    return (grad_g, grad_u, grad_d)


def input_rows(stored_gate, stored_up, gate_w, up_w):

    def term_rows(row_start, row_count):
        return jnp.dot(stored_gate, gate_w, preferred_element_type=jnp.float32) + jnp.dot(
            stored_up, up_w, preferred_element_type=jnp.float32
        )

    return term_rows


def on_device(tokens, grad_out, gate_weight, up_weight, down_weight, gate_values, chosen, counts):
    ep_count = lax.axis_size("ep")
    ep_index = lax.axis_index("ep")
    fs_index = lax.axis_index("fs")
    tok_rows = tokens.shape[0]
    quarter = tokens.shape[1]
    experts_here = chosen.shape[0]
    total_slots = ep_count * SLOTS
    live = lax.broadcasted_iota(jnp.int32, chosen.shape, 1) < counts[:, None]
    shard_of = chosen // tok_rows
    block_iota = lax.broadcasted_iota(jnp.int32, (1, 1, ep_count), 2)
    one_hot = ((shard_of[:, :, None] == block_iota) & live[:, :, None]).astype(jnp.int32)
    ranks = jnp.sum((jnp.cumsum(one_hot, axis=1) - one_hot) * one_hot, axis=2)
    slot_pos = jnp.where(live, shard_of * SLOTS + ranks, total_slots)
    expert_ids = lax.broadcasted_iota(jnp.int32, chosen.shape, 0)
    slot_token = (
        jnp.full((experts_here, total_slots), -1, jnp.int32)
        .at[expert_ids, slot_pos]
        .set(chosen, mode="drop")
    )
    own_slots = lax.dynamic_slice_in_dim(slot_token, ep_index * SLOTS, SLOTS, 1)
    has_row = own_slots >= 0
    local_rows = jnp.where(has_row, own_slots - ep_index * tok_rows, 0)
    zero_val = jnp.zeros((), tokens.dtype)
    picked_x = jnp.where(has_row[:, :, None], tokens[local_rows], zero_val)
    picked_dy = jnp.where(has_row[:, :, None], grad_out[local_rows], zero_val)
    own_pos = lax.dynamic_index_in_dim(slot_pos, fs_index, 0, keepdims=False)
    own_live = lax.dynamic_index_in_dim(live, fs_index, 0, keepdims=False)
    slot_gate = jnp.zeros((total_slots,), jnp.float32).at[own_pos].set(gate_values[0], mode="drop")
    gate_w = gate_weight[0]
    up_w = up_weight[0]
    down_w = down_weight[0]
    gathered_x, gathered_dy = (
        lax.all_gather(picked_x, "ep", axis=1, tiled=True),
        lax.all_gather(picked_dy, "ep", axis=1, tiled=True),
    )
    whole_x, whole_dy = (
        lax.all_to_all(gathered_x, "fs", split_axis=0, concat_axis=2, tiled=True),
        lax.all_to_all(gathered_dy, "fs", split_axis=0, concat_axis=2, tiled=True),
    )
    x_rows = whole_x[0]
    dy_rows = whole_dy[0]
    active, weighted, d_gate, d_up, score_term = row_products(
        x_rows, dy_rows, slot_gate, gate_w, up_w, down_w
    )
    stored = (x_rows, weighted, active, d_gate, d_up, score_term)
    term_rows = input_rows(stored[3], stored[4], gate_w, up_w)
    partial_rows = term_rows(0, total_slots)
    spread = lax.all_to_all(partial_rows[None], "fs", split_axis=2, concat_axis=0, tiled=True)
    grad_g, grad_u, grad_d = weight_grads(stored)
    returned = lax.psum_scatter(spread, "ep", scatter_dimension=1, tiled=True)
    score_sum = lax.psum(stored[5], "ep")
    safe_pos = jnp.minimum(own_pos, total_slots - 1)
    score_grad = jnp.where(own_live, score_sum[safe_pos], 0.0)[None]
    targets = jnp.where(has_row, local_rows, tok_rows).reshape(-1)
    token_sum = (
        jnp.zeros((tok_rows, quarter), jnp.float32)
        .at[targets]
        .add(returned.reshape(-1, quarter), mode="drop")
    )
    token_grad = token_sum.astype(jnp.bfloat16)
    return (
        grad_g.astype(jnp.bfloat16)[None],
        grad_u.astype(jnp.bfloat16)[None],
        grad_d.astype(jnp.bfloat16)[None],
        token_grad,
        score_grad,
    )


def solution(mesh):
    return jax.shard_map(
        on_device,
        mesh=mesh,
        in_specs=(
            P("ep", "fs"),
            P("ep", "fs"),
            P("fs", "ep", None),
            P("fs", "ep", None),
            P("fs", "ep", None),
            P("fs", None),
            P(),
            P(),
        ),
        out_specs=(
            P("fs", "ep", None),
            P("fs", "ep", None),
            P("fs", "ep", None),
            P("ep", "fs"),
            P("fs", None),
        ),
        check_vma=False,
    )
```

profile of v0, /device:TPU:2, one launch (start us, length us, event | category | flops | bytes accessed | tf_op | source)
XLA Modules:
  0.0 556.3 jit_solution(6767352351725591109)
XLA Ops:
  7.2 0.8 iota_compare_fusion.2
  10.3 2.4 reduce-window.6
  13.1 0.8 fusion.23
  13.9 0.7 and_reduce_fusion
  15.4 4.3 scatter_custom_fusion.2
  20.0 1.6 gather_fusion.1
  21.6 1.6 gather_fusion
  24.8 80.4 %all-gather.5.cloned.1.call-done = bf16[4,384,1024]{2,0,1:T(4,128)(2,1)} async-done(((bf16[4,6,1024]{2,0,1:T(4,128)(2,1)}), bf16[4,384,1024]{2,0,1:T(4,128)(2,1)}) %all-gather.5.cloned.1.call-update) | async-done | bytes 3145744 | tf_op jit(solution)/shard_map/all_gather | solution.py:85
  105.2 6.3 %copy.26 = bf16[4,384,1024]{1,2,0:T(8,128)(2,1)} copy(bf16[4,384,1024]{2,0,1:T(4,128)(2,1)} %all-gather.5.cloned.1.call-done) | data formatting | bytes 6291456 | tf_op jit(solution)/shard_map/all_gather | solution.py:85
  111.5 5.2 all-to-all-start.1
  116.7 67.2 %all-gather.3.cloned.1.call-done = bf16[4,384,1024]{2,0,1:T(4,128)(2,1)} async-done(((bf16[4,6,1024]{2,0,1:T(4,128)(2,1)}), bf16[4,384,1024]{2,0,1:T(4,128)(2,1)}) %all-gather.3.cloned.1.call-update) | async-done | bytes 3145744 | tf_op jit(solution)/shard_map/all_gather | solution.py:86
  184.0 6.3 %copy.24 = bf16[4,384,1024]{1,2,0:T(8,128)(2,1)} copy(bf16[4,384,1024]{2,0,1:T(4,128)(2,1)} %all-gather.3.cloned.1.call-done) | data formatting | bytes 6291456 | tf_op jit(solution)/shard_map/all_gather | solution.py:86
  190.2 5.2 all-to-all-start
  195.4 1.6 scatter_custom_fusion
  197.0 3.6 fusion.9
  200.6 3.0 fusion.6
  203.6 28.7 %all-to-all-done = bf16[4,384,1024]{1,2,0:T(8,128)(2,1)} async-done(((bf16[4,384,1024]{1,2,0:T(8,128)(2,1)}), bf16[4,384,1024]{1,2,0:T(8,128)(2,1)}, u32[]{:S(2)}, u32[]{:S(2)}) %all-to-all-start) | async-done | bytes 3145760 | tf_op jit(solution)/shard_map/all_to_all | solution.py:90
  232.3 3.7 multiply_reduce_fusion
  236.0 1.0 fusion.4
  237.5 3.7 add_bitcast_fusion
  241.2 14.8 %copy.27 = f32[1,384,4096]{1,0,2:T(1,128)} copy(f32[1,384,4096]{2,1,0:T(8,128)} %add_bitcast_fusion) | data formatting | bytes 12582912 | tf_op jit(solution)/shard_map/broadcast_in_dim | solution.py:100
  255.9 77.8 %all_to_all.48 = f32[1,384,4096]{1,0,2:T(1,128)} all-to-all(f32[1,384,4096]{1,0,2:T(1,128)} %copy.27), channel_id=1, replica_groups=mesh['ep'=64,'fs'=4] {'fs'}, dimensions={2} | all-to-all | bytes 12582912 | tf_op jit(solution)/shard_map/all_to_all | solution.py:100
  333.7 15.9 %copy.28 = f32[1,384,4,1024]{3,2,1,0:T(4,128)} copy(f32[1,384,4,1024]{1,0,3,2:T(1,128)} %bitcast.91) | data formatting | bytes 12582912 | tf_op jit(solution)/shard_map/all_to_all | solution.py:100
  351.6 125.2 %psum.7 = f32[384]{0:T(512)S(1)} all-reduce(f32[384]{0:T(512)S(1)} %get-tuple-element.5), channel_id=1, replica_groups=mesh['ep'=64,'fs'=4] {'ep'}, use_global_device_ids=true, to_apply=%region_8.9 | all-reduce | flops 384 | bytes 3072 | tf_op jit(solution)/shard_map/psum | solution.py:103
  476.7 1.9 gather_fusion.2
  479.3 4.4 fusion
  483.7 4.4 fusion.1
  488.0 4.6 fusion.2
  492.6 54.5 %all-reduce.3.cloned.1.call-done = f32[4,384,1024]{2,0,1:T(4,128)} async-done(((f32[4,384,1024]{2,0,1:T(4,128)}), f32[4,384,1024]{2,0,1:T(4,128)}) %all-reduce.3.cloned.1.call-update) | async-done | bytes 6291472
  547.1 0.9 constant_dynamic-slice_fusion.1
  548.1 0.9 scatter_custom_fusion.1
  549.0 0.7 convert_element_type.47
  (49 shorter events, 7.6 us)
Async XLA Ops:
  7.2 193.4 %copy-start = (bf16[1,224,4096]{2,1,0:T(8,128)(2,1)S(1)}, bf16[1,224,4096]{2,1,0:T(8,128)(2,1)}, u32[]{:S(2)}) copy-start(bf16[1,224,4096]{2,1,0:T(8,128)(2,1)} %param.10) | copy-start | bytes 5505028
  7.2 98.0 %all-gather.5.cloned.1.call-start = ((), (), s32[]{:S(2)}) async-start(), calls=%async_computation.4 | async-start | bytes 3194880 | tf_op jit(solution)/shard_map/all_gather | solution.py:85
  24.1 159.9 %all-gather.3.cloned.1.call-start = ((), (), s32[]{:S(2)}) async-start(), calls=%async_computation.3 | async-start | bytes 3194880 | tf_op jit(solution)/shard_map/all_gather | solution.py:86
  111.5 78.7 %all-to-all-start.1 = ((bf16[4,384,1024]{1,2,0:T(8,128)(2,1)}), bf16[4,384,1024]{1,2,0:T(8,128)(2,1)}, u32[]{:S(2)}, u32[]{:S(2)}) async-start(bf16[4,384,1024]{1,2,0:T(8,128)(2,1)} %copy.26), calls=%async_computation.1 | async-start | bytes 6291456 | tf_op jit(solution)/shard_map/all_to_all | solution.py:89
  190.2 42.1 %all-to-all-start = ((bf16[4,384,1024]{1,2,0:T(8,128)(2,1)}), bf16[4,384,1024]{1,2,0:T(8,128)(2,1)}, u32[]{:S(2)}, u32[]{:S(2)}) async-start(bf16[4,384,1024]{1,2,0:T(8,128)(2,1)} %copy.24), calls=%async_computation | async-start | bytes 6291456 | tf_op jit(solution)/shard_map/all_to_all | solution.py:90
  195.4 351.7 %all-reduce.3.cloned.1.call-start = ((), (), s32[]{:S(2)}) async-start(), calls=%async_computation.5 | async-start | bytes 12582912
  236.0 1.5 copy-start.2
  349.6 0.7 copy-start.3
  488.0 61.7 %copy-start.1 = (bf16[1,224,4096]{2,1,0:T(8,128)(2,1)S(1)}, bf16[1,224,4096]{2,1,0:T(8,128)(2,1)}, u32[]{:S(2)}) copy-start(bf16[1,224,4096]{2,1,0:T(8,128)(2,1)} %param.10) | copy-start | bytes 5505028
Sparse Core Ops, SparseCore 0:
  24.2 80.9 all-gather.4
  108.5 75.3 all-gather.2
  349.8 197.2 all-reduce.2
where the time goes:
time: 558 us; the launch traced here: 556 us
  waiting for transfers between devices  231 us (41%)
  blocking collectives  203 us (36%)
  local copies, waits for them, and re-layouts  59.5 us (11%)
  matrix products  28.3 us (5%)
  between operations  14.6 us (3%)
  starting transfers between devices  10.5 us (2%)
  other arithmetic  9.64 us (2%)
    psum x1, blocking collectives, on_device(): score_sum = lax.psum(stored[5], 'ep')  125 us
    all_gather x1, waiting for transfers between devices, on_device(): lax.all_gather(picked_x, 'ep', axis=1, tiled=True)  80.4 us
    all_to_all x1, blocking collectives, on_device(): lax.all_to_all(partial_rows[None], 'fs', split_axis=2, concat_axis=0, til...  77.8 us
    all_gather x1, waiting for transfers between devices, on_device(): lax.all_gather(picked_dy, 'ep', axis=1, tiled=True)  67.2 us
    unnamed x4, waiting for transfers between devices  54.6 us
    all_to_all x1, waiting for transfers between devices, on_device(): lax.all_to_all(gathered_dy, 'fs', split_axis=0, concat_axis=2, tiled=True)  28.7 us
    all_to_all x1, local copies, waits for them, and re-layouts, on_device(): lax.all_to_all(partial_rows[None], 'fs', split_axis=2, concat_axis=0, til...  15.9 us
    broadcast_in_dim x1, local copies, waits for them, and re-layouts, on_device(): partial_rows[None]  14.8 us
  transfers between devices with their start and end apart: 5, of which 4 were waited for; matrix products, arithmetic and copies ran while one was open for 7% of the time, Pallas kernels for 0%

commit v1 on v0

--- a/solution.py
+++ b/solution.py
@@ -97,7 +97,16 @@
     stored = (x_rows, weighted, active, d_gate, d_up, score_term)
     term_rows = input_rows(stored[3], stored[4], gate_w, up_w)
     partial_rows = term_rows(0, total_slots)
-    spread = lax.all_to_all(partial_rows[None], "fs", split_axis=2, concat_axis=0, tiled=True)
+    w_in = partial_rows[None]
+    spread = jnp.concatenate(
+        lax.all_to_all(
+            jnp.stack(jnp.split(w_in, lax.axis_size("fs"), 2)),
+            axis_name="fs",
+            split_axis=0,
+            concat_axis=0,
+        ),
+        axis=0,
+    )
     grad_g, grad_u, grad_d = weight_grads(stored)
     returned = lax.psum_scatter(spread, "ep", scatter_dimension=1, tiled=True)
     score_sum = lax.psum(stored[5], "ep")

time: 558 us -> 528 us (0.946)
  local copies, waits for them, and re-layouts: 59.5 us -> 36.5 us
    all_to_all x1 -> x0, local copies, waits for them, and re-layouts: 15.9 us -> none  [on_device(): lax.all_to_all(partial_rows[None], 'fs', split_axis=2, concat_axis=0, til...]
    broadcast_in_dim x1 -> x0, local copies, waits for them, and re-layouts: 14.8 us -> none  [on_device(): partial_rows[None]]
    reshape x0 -> x1, local copies, waits for them, and re-layouts: none -> 6.7 us  [on_device(): jnp.concatenate(lax.all_to_all(jnp.stack(jnp.split(w_in, lax.axis_size('f...]
where the time goes in v1:
time: 528 us; the launch traced here: 527 us
  waiting for transfers between devices  231 us (44%)
  blocking collectives  199 us (38%)
  local copies, waits for them, and re-layouts  36.5 us (7%)
  matrix products  25.6 us (5%)
  between operations  14.6 us (3%)
  starting transfers between devices  10.5 us (2%)
  other arithmetic  10.4 us (2%)
    psum x1, blocking collectives, on_device(): score_sum = lax.psum(stored[5], 'ep')  125 us
    all_gather x1, waiting for transfers between devices, on_device(): lax.all_gather(picked_x, 'ep', axis=1, tiled=True)  80.4 us
    all_to_all x1, blocking collectives, on_device(): lax.all_to_all(jnp.stack(jnp.split(w_in, lax.axis_size('fs'), 2)), axis_n...  73.7 us
    all_gather x1, waiting for transfers between devices, on_device(): lax.all_gather(picked_dy, 'ep', axis=1, tiled=True)  67.2 us
    unnamed x4, waiting for transfers between devices  54.6 us
    all_to_all x1, waiting for transfers between devices, on_device(): lax.all_to_all(gathered_dy, 'fs', split_axis=0, concat_axis=2, tiled=True)  28.7 us
  transfers between devices with their start and end apart: 5, of which 4 were waited for; matrix products, arithmetic and copies ran while one was open for 7% of the time, Pallas kernels for 0%

profile of v1, /device:TPU:2, one launch (start us, length us, event | category | flops | bytes accessed | tf_op | source)
XLA Modules:
  0.0 527.2 jit_solution(459771422427117317)
XLA Ops:
  7.2 0.8 iota_compare_fusion.2
  10.3 2.4 reduce-window.6
  13.1 0.8 fusion.23
  15.4 4.3 scatter_custom_fusion.2
  20.0 1.6 gather_fusion.1
  21.6 1.6 gather_fusion
  24.8 80.4 %all-gather.5.cloned.1.call-done = bf16[4,384,1024]{2,0,1:T(4,128)(2,1)} async-done(((bf16[4,6,1024]{2,0,1:T(4,128)(2,1)}), bf16[4,384,1024]{2,0,1:T(4,128)(2,1)}) %all-gather.5.cloned.1.call-update) | async-done | bytes 3145744 | tf_op jit(solution)/shard_map/all_gather | solution.py:85
  105.2 6.3 %copy.24 = bf16[4,384,1024]{1,2,0:T(8,128)(2,1)} copy(bf16[4,384,1024]{2,0,1:T(4,128)(2,1)} %all-gather.5.cloned.1.call-done) | data formatting | bytes 6291456 | tf_op jit(solution)/shard_map/all_gather | solution.py:85
  111.5 5.2 all-to-all-start.1
  116.7 67.2 %all-gather.3.cloned.1.call-done = bf16[4,384,1024]{2,0,1:T(4,128)(2,1)} async-done(((bf16[4,6,1024]{2,0,1:T(4,128)(2,1)}), bf16[4,384,1024]{2,0,1:T(4,128)(2,1)}) %all-gather.3.cloned.1.call-update) | async-done | bytes 3145744 | tf_op jit(solution)/shard_map/all_gather | solution.py:86
  184.0 6.3 %copy.22 = bf16[4,384,1024]{1,2,0:T(8,128)(2,1)} copy(bf16[4,384,1024]{2,0,1:T(4,128)(2,1)} %all-gather.3.cloned.1.call-done) | data formatting | bytes 6291456 | tf_op jit(solution)/shard_map/all_gather | solution.py:86
  190.2 5.2 all-to-all-start
  195.4 1.6 scatter_custom_fusion
  197.0 3.6 fusion.9
  200.6 3.0 fusion.6
  203.6 28.7 %all-to-all-done = bf16[4,384,1024]{1,2,0:T(8,128)(2,1)} async-done(((bf16[4,384,1024]{1,2,0:T(8,128)(2,1)}), bf16[4,384,1024]{1,2,0:T(8,128)(2,1)}, u32[]{:S(2)}, u32[]{:S(2)}) %all-to-all-start) | async-done | bytes 3145760 | tf_op jit(solution)/shard_map/all_to_all | solution.py:90
  232.3 3.7 multiply_reduce_fusion
  236.0 1.0 fusion.4
  237.5 1.0 add_bitcast_fusion
  238.5 1.0 slice_bitcast_fusion.3
  239.5 0.8 pad_maximum_fusion
  240.3 73.7 %all_to_all.35 = f32[4,1,384,1024]{3,2,1,0:T(8,128)S(1)} all-to-all(f32[4,1,384,1024]{3,2,1,0:T(8,128)S(1)} %pad_maximum_fusion), channel_id=1, replica_groups=mesh['ep'=64,'fs'=4] {'fs'}, dimensions={0} | all-to-all | bytes 12582912 | tf_op jit(solution)/shard_map/all_to_all | solution.py:102
  314.0 6.7 %copy.25 = f32[4,384,1024]{2,0,1:T(4,128)} copy(f32[4,384,1024]{2,1,0:T(8,128)S(1)} %bitcast.95) | data formatting | bytes 12582912 | tf_op jit(solution)/shard_map/reshape | solution.py:101
  322.6 125.0 %psum.7 = f32[384]{0:T(512)S(1)} all-reduce(f32[384]{0:T(512)S(1)} %get-tuple-element.5), channel_id=1, replica_groups=mesh['ep'=64,'fs'=4] {'ep'}, use_global_device_ids=true, to_apply=%region_8.9 | all-reduce | flops 384 | bytes 3072 | tf_op jit(solution)/shard_map/psum | solution.py:112
  447.6 1.9 gather_fusion.2
  450.2 4.4 fusion
  454.6 4.4 fusion.1
  458.9 4.6 fusion.2
  463.5 54.5 %all-reduce.3.cloned.1.call-done = f32[4,384,1024]{2,0,1:T(4,128)} async-done(((f32[4,384,1024]{2,0,1:T(4,128)}), f32[4,384,1024]{2,0,1:T(4,128)}) %all-reduce.3.cloned.1.call-update) | async-done | bytes 6291472
  518.0 0.9 constant_dynamic-slice_fusion.1
  519.0 0.9 scatter_custom_fusion.1
  519.9 0.7 convert_element_type.47
  (50 shorter events, 8.4 us)
Async XLA Ops:
  7.2 193.4 %copy-start = (bf16[1,224,4096]{2,1,0:T(8,128)(2,1)S(1)}, bf16[1,224,4096]{2,1,0:T(8,128)(2,1)}, u32[]{:S(2)}) copy-start(bf16[1,224,4096]{2,1,0:T(8,128)(2,1)} %param.10) | copy-start | bytes 5505028
  7.2 98.0 %all-gather.5.cloned.1.call-start = ((), (), s32[]{:S(2)}) async-start(), calls=%async_computation.4 | async-start | bytes 3194880 | tf_op jit(solution)/shard_map/all_gather | solution.py:85
  24.1 159.9 %all-gather.3.cloned.1.call-start = ((), (), s32[]{:S(2)}) async-start(), calls=%async_computation.3 | async-start | bytes 3194880 | tf_op jit(solution)/shard_map/all_gather | solution.py:86
  111.5 78.7 %all-to-all-start.1 = ((bf16[4,384,1024]{1,2,0:T(8,128)(2,1)}), bf16[4,384,1024]{1,2,0:T(8,128)(2,1)}, u32[]{:S(2)}, u32[]{:S(2)}) async-start(bf16[4,384,1024]{1,2,0:T(8,128)(2,1)} %copy.24), calls=%async_computation.1 | async-start | bytes 6291456 | tf_op jit(solution)/shard_map/all_to_all | solution.py:89
  190.2 42.1 %all-to-all-start = ((bf16[4,384,1024]{1,2,0:T(8,128)(2,1)}), bf16[4,384,1024]{1,2,0:T(8,128)(2,1)}, u32[]{:S(2)}, u32[]{:S(2)}) async-start(bf16[4,384,1024]{1,2,0:T(8,128)(2,1)} %copy.22), calls=%async_computation | async-start | bytes 6291456 | tf_op jit(solution)/shard_map/all_to_all | solution.py:90
  195.4 322.6 %all-reduce.3.cloned.1.call-start = ((), (), s32[]{:S(2)}) async-start(), calls=%async_computation.5 | async-start | bytes 12582912
  236.0 1.5 copy-start.2
  320.7 0.7 copy-start.3
  458.9 61.7 %copy-start.1 = (bf16[1,224,4096]{2,1,0:T(8,128)(2,1)S(1)}, bf16[1,224,4096]{2,1,0:T(8,128)(2,1)}, u32[]{:S(2)}) copy-start(bf16[1,224,4096]{2,1,0:T(8,128)(2,1)} %param.10) | copy-start | bytes 5505028
Sparse Core Ops, SparseCore 0:
  24.2 80.9 all-gather.4
  108.5 75.3 all-gather.2
  320.8 197.1 all-reduce.2
